TPU v7x, 32 devices: a whole 2x2x4 slice. The times are simulated.
32 devices in a mesh: cache: 8 (over z, x), owner: 4 (over y, core).
Axes of the slice: x: 2, y: 2, z: 4, core: 2. Of those that a mesh axis runs over, the one named last changes fastest.
Arguments:
- cache: bfloat16 [32, 4, 128, 256], P('cache'), may hold values from -2.5 to 2.5
- backing: bfloat16 [32, 32, 128, 256], P('cache', 'owner'), may hold values from -2.5 to 2.5
- resident: int32 [32, 4], P('cache'), may hold values from 0 to 31, as said below
- promote: int32 [32, 2], P('cache'), may hold values from 0 to 31, as said below
- victim: int32 [32, 2], P('cache'), may hold values from 0 to 3, as said below
- lookups: int32 [2, 4096, 32, 8], P(None, 'owner', 'cache'), may hold values from 0 to 511
- route: int32 [2, 4, 1024], P(None, 'owner'), may hold values from 0 to 1023, each once within a row
- dcn_down: bfloat16 [8192, 128], P('cache'), may hold values from -0.0625 to 0.0625
- dcn_up: bfloat16 [128, 8192], P(None, 'cache'), may hold values from -0.5 to 0.5
- dcn_bias: float32 [8192], replicated, may hold values from -5 to 5
- mlp_in: bfloat16 [8192, 1024], P('cache'), may hold values from -0.0625 to 0.0625
- mlp_bias: float32 [1024], replicated, may hold values from -3 to 3
- mlp_out: float32 [1024], replicated, may hold values from -0.1875 to 0.1875
- out_bias: float32 [1], replicated, may hold values from -4 to 4
Outputs:
- scores: float32 [2, 4, 1024], P(None, 'owner', 'cache')
- new_cache: bfloat16 [32, 4, 128, 256], P('cache')
- new_backing: bfloat16 [32, 32, 128, 256], P('cache', 'owner')
Inputs may be any that keep to these rules, and one draw needn't show every extreme that they name: `resident`: for each feature, 4 distinct backing blocks. `promote`: for each feature, 2 distinct backing blocks, none of them in that feature's resident; block k belongs to owner k // 8. `victim`: for each feature, 2 distinct slots. `route`: each batch and owner group holds every request index once.
All inputs are finite; a program needn't handle non-finite values.
Results may differ from a plain program's by a relative error of at most 0.004.
Values may be sent and summed in bfloat16 or wider, within the bound.
A program may use at most 128 MiB of HBM per device.

v0:
```python
import jax
import jax.numpy as jnp
from jax import lax
from jax.sharding import PartitionSpec as P


def take_rows(table, wanted):
    return jax.vmap(lambda rows, chosen: rows[chosen])(table, wanted)


def pool_batch(requests, order, table):
    requests = requests[order]
    count = requests.shape[0]
    step = min(512, count)
    codes = jnp.arange(table.shape[1], dtype=jnp.int32)

    def one_block(lookup_block):
        counts = jnp.sum((lookup_block[..., None] == codes).astype(jnp.bfloat16), axis=2)
        return jnp.einsum("rfk,fke->rfe", counts, table, preferred_element_type=jnp.float32).astype(
            jnp.bfloat16
        )

    blocks = requests.reshape((count // step, step) + requests.shape[1:])
    pooled = lax.map(one_block, blocks)
    return pooled.reshape((count,) + pooled.shape[2:])


def on_device(
    cache,
    backing,
    resident,
    promote,
    victim,
    lookups,
    route,
    dcn_down,
    dcn_up,
    dcn_bias,
    mlp_in,
    mlp_bias,
    mlp_out,
    out_bias,
):
    held = cache.shape[0]
    slots = cache.shape[1]
    block = cache.shape[2]
    width = cache.shape[3]
    own_blocks = backing.shape[1]
    promoted_count = promote.shape[1]
    owner_here = lax.axis_index("owner")
    local_index = promote - owner_here * own_blocks
    owned_here = (local_index >= 0) & (local_index < own_blocks)
    clamped = jnp.clip(local_index, 0, own_blocks - 1)
    fetched = take_rows(backing, clamped)
    outgoing = jnp.where(owned_here[:, :, None, None], fetched, jnp.zeros_like(fetched))
    arrived = lax.all_gather(outgoing, "owner", axis=0, tiled=True)
    owners = arrived.shape[0] // held
    arrived = arrived.reshape(owners, held, promoted_count, block, width)
    source = promote // own_blocks
    picked = source[None] == jnp.arange(owners, dtype=jnp.int32)[:, None, None]
    promoted = jnp.sum(jnp.where(picked[..., None, None], arrived, jnp.zeros_like(arrived)), axis=0)
    evicted = take_rows(cache, victim)
    leaving = take_rows(resident, victim) - owner_here * own_blocks
    slot_numbers = jnp.arange(slots, dtype=jnp.int32)
    block_numbers = jnp.arange(own_blocks, dtype=jnp.int32)
    new_cache = cache
    new_backing = backing
    for column in range(promoted_count):
        slot_hit = victim[:, column][:, None] == slot_numbers[None, :]
        new_cache = jnp.where(slot_hit[:, :, None, None], promoted[:, column][:, None], new_cache)
        block_hit = leaving[:, column][:, None] == block_numbers[None, :]
        new_backing = jnp.where(
            block_hit[:, :, None, None], evicted[:, column][:, None], new_backing
        )
    table = new_cache.reshape(held, slots * block, width)
    batches = lookups.shape[0]
    received = []
    for batch_turn in range(batches):
        pooled = pool_batch(lookups[batch_turn], route[batch_turn, 0], table)
        received.append(lax.all_to_all(pooled, "cache", split_axis=0, concat_axis=1, tiled=True))
    arrived_rows = jnp.stack(received)
    per_batch = arrived_rows.shape[1]
    features = arrived_rows.reshape(batches * per_batch, -1)
    low = jnp.dot(
        features,
        lax.all_gather(dcn_down, "cache", axis=0, tiled=True),
        preferred_element_type=jnp.float32,
    ).astype(jnp.bfloat16)
    gate = (
        jnp.dot(
            low,
            lax.all_gather(dcn_up, "cache", axis=1, tiled=True),
            preferred_element_type=jnp.float32,
        )
        + dcn_bias
    )
    crossed = (features * gate + features).astype(jnp.bfloat16)
    portion = mlp_in.shape[1] // lax.axis_size("owner")
    own_columns = lax.dynamic_slice_in_dim(mlp_in, owner_here * portion, portion, 1)
    column_block = lax.all_gather(own_columns, "cache", axis=0, tiled=True)
    before = jnp.dot(
        crossed,
        lax.all_gather(column_block, "owner", axis=1, tiled=True),
        preferred_element_type=jnp.float32,
    )
    hidden = jnp.maximum(before + mlp_bias, 0.0)
    scores = jnp.sum(hidden * mlp_out, axis=-1) + out_bias[0]
    return (scores.reshape(batches, 1, per_batch), new_cache, new_backing)


def solution(mesh):
    in_specs = (
        P("cache", None, None, None),
        P("cache", "owner", None, None),
        P("cache", None),
        P("cache", None),
        P("cache", None),
        P(None, "owner", "cache", None),
        P(None, "owner", None),
        P("cache", None),
        P(None, "cache"),
        P(),
        P("cache", None),
        P(),
        P(),
        P(),
    )
    out_specs = (
        P(None, "owner", "cache"),
        P("cache", None, None, None),
        P("cache", "owner", None, None),
    )
    return jax.shard_map(
        on_device, mesh=mesh, in_specs=in_specs, out_specs=out_specs, check_vma=False
    )
```

profile of v0, /device:TPU:0, one launch (start us, length us, event | category | flops | bytes accessed | tf_op | source)
XLA Modules:
  0.0 392.6 jit_solution(9065323531690684591)
XLA Ops:
  7.2 1.5 copy-done
  8.8 0.9 constant_dynamic-slice_fusion
  9.7 0.7 fusion.37
  10.6 0.7 compare_and_fusion
  11.4 2.2 gather_fusion.2
  13.6 0.9 broadcast_select_fusion
  14.5 0.7 all-gather.8.cloned.1.call-update
  15.8 70.4 %all-gather.12.cloned.1.call-done = bf16[8192,256]{1,0:T(8,128)(2,1)} async-done(((bf16[1024,256]{1,0:T(8,128)(2,1)}), bf16[8192,256]{1,0:T(8,128)(2,1)}) %all-gather.12.cloned.1.call-update) | async-done | bytes 4194320 | tf_op jit(solution)/shard_map/all_gather | solution.py:100
  86.3 0.6 copy-done.9
  87.2 0.8 copy.137
  88.1 7.9 %gather_fusion = s32[1024,4,8]{2,1,0:T(4,128)} fusion(s32[1024,4,8]{2,1,0:T(4,128)S(1)} %bitcast.100, s32[1024]{0:T(1024)S(1)} %broadcast_clamp_fusion.1), kind=kCustom, calls=%fused_computation | custom fusion | bytes 266240 | tf_op jit(solution)/shard_map/gather | solution.py:12
  96.0 1.8 copy.113
  98.0 10.9 %all-gather.6.cloned.1.call-done = bf16[16,2,128,256]{3,2,1,0:T(8,128)(2,1)} async-done(((bf16[4,2,128,256]{3,2,1,0:T(8,128)(2,1)}), bf16[16,2,128,256]{3,2,1,0:T(8,128)(2,1)}) %all-gather.6.cloned.1.call-update) | async-done | bytes 2097168 | tf_op jit(solution)/shard_map/all_gather | solution.py:56
  108.9 2.1 select_reduce_fusion
  111.1 1.2 select_select_fusion.1
  112.3 1.5 broadcast.130.clone2.1
  113.7 27.7 %while.26 = (s32[]{:T(128)}, bf16[2,512,4,256]{3,1,0,2:T(8,128)(2,1)}, s32[2,512,4,8]{1,3,2,0:T(8,128)S(1)}, bf16[4,512,256]{2,1,0:T(8,128)(2,1)}, s32[]{:T(128)}) while((s32[]{:T(128)}, bf16[2,512,4,256]{3,1,0,2:T(8,128)(2,1)}, s32[2,512,4,8]{1,3,2,0:T(8,128)S(1)}, bf16[4,512,256]{2,1,0:T(8,128)(2,1)}, s32[]{:T(128)}) %tuple.91), condition=%wide.region_3.4_spmd.clone, body=%wide.region_1.3_spmd.clone.sunk | while | flops 561512448 | bytes 10814045 | solution.py:24
  114.2 11.7 %fusion.60 = bf16[512,4,512]{2,1,0:T(4,128)(2,1)S(1)} fusion(s32[512,4,8]{2,1,0:T(4,128)S(1)} %copy.164), kind=kLoop, calls=%fused_computation.9.clone.1 | loop fusion | flops 24117248 | bytes 2162688 | tf_op jit(solution)/shard_map/while/body/eval_jaxpr/reduce_sum | solution.py:18
  125.9 1.7 fusion.61
  128.0 11.7 %fusion.60 = bf16[512,4,512]{2,1,0:T(4,128)(2,1)S(1)} fusion(s32[512,4,8]{2,1,0:T(4,128)S(1)} %copy.164), kind=kLoop, calls=%fused_computation.9.clone.1 | loop fusion | flops 24117248 | bytes 2162688 | tf_op jit(solution)/shard_map/while/body/eval_jaxpr/reduce_sum | solution.py:18
  139.8 1.7 fusion.61
  141.5 4.5 %copy.115 = bf16[1024,4,256]{2,1,0:T(4,128)(2,1)} copy(bf16[1024,4,256]{2,0,1:T(8,128)(2,1)} %bitcast.12) | data formatting | bytes 4194304 | tf_op jit(solution)/shard_map/reshape | solution.py:25
  146.0 5.5 %all-to-all-start = ((bf16[1024,4,256]{2,1,0:T(4,128)(2,1)}), bf16[1024,4,256]{2,1,0:T(4,128)(2,1)}, u32[]{:S(2)}, u32[]{:S(2)}) async-start(bf16[1024,4,256]{2,1,0:T(4,128)(2,1)} %copy.115), calls=%async_computation | async-start | bytes 4194304 | tf_op jit(solution)/shard_map/all_to_all | solution.py:80
  151.5 0.8 copy.138
  152.3 7.9 %gather_fusion.1 = s32[1024,4,8]{2,1,0:T(4,128)} fusion(s32[1024,4,8]{2,1,0:T(4,128)S(1)} %bitcast.101, s32[1024]{0:T(1024)S(1)} %broadcast_clamp_fusion), kind=kCustom, calls=%fused_computation.1 | custom fusion | bytes 266240 | tf_op jit(solution)/shard_map/gather | solution.py:12
  160.3 1.8 copy.120
  162.1 1.5 broadcast.130.clone2
  163.6 27.7 %while.27 = (s32[]{:T(128)}, bf16[2,512,4,256]{3,1,0,2:T(8,128)(2,1)}, s32[2,512,4,8]{1,3,2,0:T(8,128)S(1)}, bf16[4,512,256]{2,1,0:T(8,128)(2,1)}, s32[]{:T(128)}) while((s32[]{:T(128)}, bf16[2,512,4,256]{3,1,0,2:T(8,128)(2,1)}, s32[2,512,4,8]{1,3,2,0:T(8,128)S(1)}, bf16[4,512,256]{2,1,0:T(8,128)(2,1)}, s32[]{:T(128)}) %tuple.92), condition=%wide.region_6.7_spmd.clone, body=%wide.region_4.6_spmd.clone.sunk | while | flops 561512448 | bytes 10814045 | solution.py:24
  164.0 11.7 %fusion.64 = bf16[512,4,512]{2,1,0:T(4,128)(2,1)S(1)} fusion(s32[512,4,8]{2,1,0:T(4,128)S(1)} %copy.166), kind=kLoop, calls=%fused_computation.18.clone.1 | loop fusion | flops 24117248 | bytes 2162688 | tf_op jit(solution)/shard_map/while/body/eval_jaxpr/reduce_sum | solution.py:18
  175.7 1.7 fusion.65
  177.9 11.7 %fusion.64 = bf16[512,4,512]{2,1,0:T(4,128)(2,1)S(1)} fusion(s32[512,4,8]{2,1,0:T(4,128)S(1)} %copy.166), kind=kLoop, calls=%fused_computation.18.clone.1 | loop fusion | flops 24117248 | bytes 2162688 | tf_op jit(solution)/shard_map/while/body/eval_jaxpr/reduce_sum | solution.py:18
  189.6 1.7 fusion.65
  191.3 4.6 %copy.122 = bf16[1024,4,256]{2,1,0:T(4,128)(2,1)} copy(bf16[1024,4,256]{2,0,1:T(8,128)(2,1)} %bitcast.20) | data formatting | bytes 4194304 | tf_op jit(solution)/shard_map/reshape | solution.py:25
  195.9 17.7 %all-to-all-done = bf16[1024,4,256]{2,1,0:T(4,128)(2,1)} async-done(((bf16[1024,4,256]{2,1,0:T(4,128)(2,1)}), bf16[1024,4,256]{2,1,0:T(4,128)(2,1)}, u32[]{:S(2)}, u32[]{:S(2)}) %all-to-all-start) | async-done | bytes 2097184 | tf_op jit(solution)/shard_map/all_to_all | solution.py:80
  213.6 4.6 %all-to-all-start.1 = ((bf16[1024,4,256]{2,1,0:T(4,128)(2,1)}), bf16[1024,4,256]{2,1,0:T(4,128)(2,1)}, u32[]{:S(2)}, u32[]{:S(2)}) async-start(bf16[1024,4,256]{2,1,0:T(4,128)(2,1)} %copy.122), calls=%async_computation.1 | async-start | bytes 4194304 | tf_op jit(solution)/shard_map/all_to_all | solution.py:80
  219.0 0.6 gather_fusion.4
  219.6 0.7 gather_fusion.3
  220.7 3.3 select_select_fusion
  224.0 1.9 copy.116
  225.8 1.6 copy.117
  227.4 53.9 %all-to-all-done.1 = bf16[1024,4,256]{2,1,0:T(4,128)(2,1)} async-done(((bf16[1024,4,256]{2,1,0:T(4,128)(2,1)}), bf16[1024,4,256]{2,1,0:T(4,128)(2,1)}, u32[]{:S(2)}, u32[]{:S(2)}) %all-to-all-start.1) | async-done | bytes 2097184 | tf_op jit(solution)/shard_map/all_to_all | solution.py:80
  281.3 1.9 copy.123
  283.4 1.5 copy-done.3
  285.3 2.4 copy.125
  287.7 6.3 %copy.142 = bf16[32,8,32,256]{3,1,2,0:T(8,128)(2,1)} copy(bf16[32,8,32,256]{3,2,1,0:T(8,128)(2,1)S(1)} %bitcast.99) | data formatting | bytes 8388608
  294.0 4.3 %convolution_convert_fusion = bf16[256,128]{1,0:T(8,128)(2,1)S(1)} fusion(bf16[256,8192]{1,0:T(8,128)(2,1)} %bitcast.97, bf16[8192,128]{1,0:T(8,128)(2,1)} %all-gather.8.cloned.1.call-done), kind=kOutput, calls=%fused_computation.35 | convolution fusion | flops 536903680 | bytes 6356992 | tf_op jit(solution)/shard_map/dot_general | solution.py:84
  298.3 74.4 %all-gather.14.cloned.1.call-done = bf16[8192,1024]{1,0:T(8,128)(2,1)} async-done(((bf16[8192,256]{1,0:T(8,128)(2,1)}), bf16[8192,1024]{1,0:T(8,128)(2,1)}) %all-gather.14.cloned.1.call-update) | async-done | bytes 16777232 | tf_op jit(solution)/shard_map/all_gather | solution.py:103
  372.7 12.8 %fusion.33 = f32[256]{0:T(256)S(1)} fusion(bf16[8192,1024]{1,0:T(8,128)(2,1)} %all-gather.14.cloned.1.call-done, bf16[256,128]{1,0:T(8,128)(2,1)S(1)} %convolution_convert_fusion, bf16[128,8192]{1,0:T(8,128)(2,1)} %all-gather.10.cloned.1.call-done, bf16[256,8192]{1,0:T(8,128)(2,1)} %bitcast.98, f32[8192]{0:T(1024)S(1)} %copy-done.12, ...), kind=kOutput, calls=%fused_computation.34 | convolution fusion | flops 4843372544 | bytes 23176192 | tf_op jit(solution)/shard_map/dot_general | solution.py:101
  (74 shorter events, 4.9 us)
Async XLA Ops:
  7.2 1.6 copy-start
  7.2 79.0 %all-gather.12.cloned.1.call-start = ((), (), s32[]{:S(2)}) async-start(), calls=%async_computation.5 | async-start | bytes 4718592 | tf_op jit(solution)/shard_map/all_gather | solution.py:100
  9.6 99.3 %all-gather.6.cloned.1.call-start = ((), (), s32[]{:S(2)}) async-start(), calls=%async_computation.2 | async-start | bytes 2621440 | tf_op jit(solution)/shard_map/all_gather | solution.py:56
  14.5 279.5 %all-gather.8.cloned.1.call-start = ((), (), s32[]{:S(2)}) async-start(), calls=%async_computation.3 | async-start | bytes 2359296 | tf_op jit(solution)/shard_map/all_gather | solution.py:86
  15.2 283.1 %all-gather.10.cloned.1.call-start = ((), (), s32[]{:S(2)}) async-start(), calls=%async_computation.4 | async-start | bytes 2359296 | tf_op jit(solution)/shard_map/all_gather | solution.py:92
  15.8 356.9 %all-gather.14.cloned.1.call-start = ((), (), s32[]{:S(2)}) async-start(), calls=%async_computation.6 | async-start | bytes 20971520 | tf_op jit(solution)/shard_map/all_gather | solution.py:103
  86.2 0.7 copy-start.9
  86.2 1.0 copy-start.8
  86.3 1.8 copy-start.10
  96.0 1.9 copy-start.11
  97.9 13.2 %copy-start.4 = (bf16[4,4,128,256]{3,2,1,0:T(8,128)(2,1)S(1)}, bf16[4,4,128,256]{3,2,1,0:T(8,128)(2,1)}, u32[]{:S(2)}) copy-start(bf16[4,4,128,256]{3,2,1,0:T(8,128)(2,1)} %param.18) | copy-start | bytes 3145732
  114.2 11.7 %copy-start.6 = (bf16[4,512,256]{2,1,0:T(8,128)(2,1)S(1)}, bf16[4,512,256]{2,1,0:T(8,128)(2,1)}, u32[]{:S(2)}) copy-start(bf16[4,512,256]{2,1,0:T(8,128)(2,1)} %get-tuple-element.305) | copy-start | bytes 3145732 | tf_op jit(solution)/shard_map/while
  128.0 11.7 %copy-start.6 = (bf16[4,512,256]{2,1,0:T(8,128)(2,1)S(1)}, bf16[4,512,256]{2,1,0:T(8,128)(2,1)}, u32[]{:S(2)}) copy-start(bf16[4,512,256]{2,1,0:T(8,128)(2,1)} %get-tuple-element.305) | copy-start | bytes 3145732 | tf_op jit(solution)/shard_map/while
  146.0 67.6 %all-to-all-start = ((bf16[1024,4,256]{2,1,0:T(4,128)(2,1)}), bf16[1024,4,256]{2,1,0:T(4,128)(2,1)}, u32[]{:S(2)}, u32[]{:S(2)}) async-start(bf16[1024,4,256]{2,1,0:T(4,128)(2,1)} %copy.115), calls=%async_computation | async-start | bytes 4194304 | tf_op jit(solution)/shard_map/all_to_all | solution.py:80
  164.0 11.7 %copy-start.7 = (bf16[4,512,256]{2,1,0:T(8,128)(2,1)S(1)}, bf16[4,512,256]{2,1,0:T(8,128)(2,1)}, u32[]{:S(2)}) copy-start(bf16[4,512,256]{2,1,0:T(8,128)(2,1)} %get-tuple-element.290) | copy-start | bytes 3145732 | tf_op jit(solution)/shard_map/while
  177.8 11.7 %copy-start.7 = (bf16[4,512,256]{2,1,0:T(8,128)(2,1)S(1)}, bf16[4,512,256]{2,1,0:T(8,128)(2,1)}, u32[]{:S(2)}) copy-start(bf16[4,512,256]{2,1,0:T(8,128)(2,1)} %get-tuple-element.290) | copy-start | bytes 3145732 | tf_op jit(solution)/shard_map/while
  195.9 23.1 %copy-start.5 = (bf16[4,4,128,256]{3,2,1,0:T(8,128)(2,1)S(1)}, bf16[4,4,128,256]{3,2,1,0:T(8,128)(2,1)}, u32[]{:S(2)}) copy-start(bf16[4,4,128,256]{3,2,1,0:T(8,128)(2,1)} %param.18) | copy-start | bytes 3145732
  195.9 23.7 %copy-start.2 = (s32[4,4]{1,0:T(4,128)S(1)}, s32[4,4]{1,0:T(4,128)}, u32[]{:S(2)}) copy-start(s32[4,4]{1,0:T(4,128)} %param.20) | copy-start | bytes 196
  213.6 67.7 %all-to-all-start.1 = ((bf16[1024,4,256]{2,1,0:T(4,128)(2,1)}), bf16[1024,4,256]{2,1,0:T(4,128)(2,1)}, u32[]{:S(2)}, u32[]{:S(2)}) async-start(bf16[1024,4,256]{2,1,0:T(4,128)(2,1)} %copy.122), calls=%async_computation.1 | async-start | bytes 4194304 | tf_op jit(solution)/shard_map/all_to_all | solution.py:80
  283.2 1.6 copy-start.3
  294.0 78.7 %copy-start.12 = (f32[8192]{0:T(1024)S(1)}, f32[8192]{0:T(1024)}, u32[]{:S(2)}) copy-start(f32[8192]{0:T(1024)} %param.27) | copy-start | bytes 98308
  294.0 78.7 %copy-start.13 = (f32[1024]{0:T(1024)S(1)}, f32[1024]{0:T(1024)}, u32[]{:S(2)}) copy-start(f32[1024]{0:T(1024)} %param.30) | copy-start | bytes 12292
  294.0 78.7 %copy-start.14 = (f32[1024]{0:T(1024)S(1)}, f32[1024]{0:T(1024)}, u32[]{:S(2)}) copy-start(f32[1024]{0:T(1024)} %param.29) | copy-start | bytes 12292
  372.7 13.3 %copy-start.1 = (bf16[1024,1024]{1,0:T(8,128)(2,1)S(1)}, bf16[1024,1024]{1,0:T(8,128)(2,1)}, u32[]{:S(2)}) copy-start(bf16[1024,1024]{1,0:T(8,128)(2,1)} %param.28) | copy-start | bytes 6291460
Sparse Core Ops, SparseCore 0:
  10.7 75.4 all-gather.11
  87.8 21.0 all-gather.5
  111.1 52.2 all-gather.7
  165.3 89.3 all-gather.9
  256.1 116.5 all-gather.13
where the time goes:
time: 393 us
  waiting for transfers between devices  229 us (58%)
  local copies, waits for them, and re-layouts  58.2 us (15%)
  other arithmetic  56.9 us (14%)
  matrix products  23.8 us (6%)
  between operations  14.7 us (4%)
  starting transfers between devices  10.3 us (3%)
    all_gather x1, waiting for transfers between devices, on_device(): lax.all_gather(column_block, 'owner', axis=1, tiled=True)  74.4 us
    all_to_all x2, waiting for transfers between devices, on_device(): lax.all_to_all(pooled, 'cache', split_axis=0, concat_axis=1, tiled=True)  71.6 us
    all_gather x1, waiting for transfers between devices, on_device(): column_block = lax.all_gather(own_columns, 'cache', axis=0, tiled=True)  70.4 us
    reduce_sum x4, other arithmetic, one_block(): jnp.sum((lookup_block[..., None] == codes).astype(jnp.bfloat16), axis=2)  46.9 us
    gather x2, local copies, waits for them, and re-layouts, pool_batch(): requests = requests[order]  15.9 us
    unnamed x31, local copies, waits for them, and re-layouts  15.5 us
    dot_general x1, matrix products, on_device(): jnp.dot(crossed, lax.all_gather(column_block, 'owner', axis=1, tiled=True...  12.8 us
    all_gather x1, waiting for transfers between devices, on_device(): arrived = lax.all_gather(outgoing, 'owner', axis=0, tiled=True)  10.9 us
  transfers between devices with their start and end apart: 7, of which 5 were waited for; matrix products, arithmetic and copies ran while one was open for 31% of the time, Pallas kernels for 0%

commit v1 on v0

--- a/solution.py
+++ b/solution.py
@@ -97,7 +97,14 @@
     crossed = (features * gate + features).astype(jnp.bfloat16)
     portion = mlp_in.shape[1] // lax.axis_size("owner")
     own_columns = lax.dynamic_slice_in_dim(mlp_in, owner_here * portion, portion, 1)
-    column_block = lax.all_gather(own_columns, "cache", axis=0, tiled=True)
+    ring = [own_columns]
+    for hop in range(7):
+        ring.append(lax.ppermute(ring[-1], "cache", [(dev, (dev + 1) % 8) for dev in range(8)]))
+    column_block = jnp.roll(
+        jnp.concatenate(ring[::-1], axis=0),
+        (lax.axis_index("cache") + 1) * ring[0].shape[0],
+        axis=0,
+    )
     before = jnp.dot(
         crossed,
         lax.all_gather(column_block, "owner", axis=1, tiled=True),

time: 393 us -> 333 us (0.85)
  waiting for transfers between devices: 229 us -> 167 us
    ppermute x0 -> x7, waiting for transfers between devices: none -> 129 us  [on_device(): lax.ppermute(ring[-1], 'cache', [(dev, (dev + 1) % 8) for dev in range(8)])]
    all_gather x1, waiting for transfers between devices: 74.4 us -> 0.02 us  [on_device(): lax.all_gather(column_block, 'owner', axis=1, tiled=True)]
    all_gather x1 -> x0, waiting for transfers between devices: 70.4 us -> none  [on_device(): column_block = lax.all_gather(own_columns, 'cache', axis=0, tiled=True)]
    all_to_all x2, waiting for transfers between devices: 71.6 us -> 37.8 us  [on_device(): lax.all_to_all(pooled, 'cache', split_axis=0, concat_axis=1, tiled=True)]
    all_gather x1, waiting for transfers between devices: 10.9 us -> 0.02 us  [on_device(): arrived = lax.all_gather(outgoing, 'owner', axis=0, tiled=True)]
    unnamed x31 -> x44, local copies, waits for them, and re-layouts: 15.5 us -> 16.5 us
  transfers between devices with their start and end apart: 7 -> 13, of which waited for: 5 -> 9; matrix products, arithmetic and copies ran while one was open for 31% -> 35% of each run, Pallas kernels for 0% -> 0%
where the time goes in v1:
time: 333 us; the launch traced here: 332 us
  waiting for transfers between devices  167 us (50%)
  other arithmetic  56.9 us (17%)
  local copies, waits for them, and re-layouts  55.8 us (17%)
  matrix products  24.8 us (7%)
  between operations  14.8 us (4%)
  starting transfers between devices  12 us (4%)
    ppermute x7, waiting for transfers between devices, on_device(): lax.ppermute(ring[-1], 'cache', [(dev, (dev + 1) % 8) for dev in range(8)])  129 us
    reduce_sum x4, other arithmetic, one_block(): jnp.sum((lookup_block[..., None] == codes).astype(jnp.bfloat16), axis=2)  46.9 us
    all_to_all x2, waiting for transfers between devices, on_device(): lax.all_to_all(pooled, 'cache', split_axis=0, concat_axis=1, tiled=True)  37.8 us
    unnamed x44, local copies, waits for them, and re-layouts  16.5 us
    gather x2, local copies, waits for them, and re-layouts, pool_batch(): requests = requests[order]  15.8 us
    dot_general x1, matrix products, on_device(): jnp.dot(crossed, lax.all_gather(column_block, 'owner', axis=1, tiled=True...  12.7 us
    all_to_all x2, starting transfers between devices, on_device(): lax.all_to_all(pooled, 'cache', split_axis=0, concat_axis=1, tiled=True)  8.83 us
    dot_general x4, matrix products, one_block(): jnp.einsum('rfk,fke->rfe', counts, table, preferred_element_type=jnp.floa...  7.99 us
  transfers between devices with their start and end apart: 13, of which 9 were waited for; matrix products, arithmetic and copies ran while one was open for 35% of the time, Pallas kernels for 0%

profile of v1, /device:TPU:0, one launch (start us, length us, event | category | flops | bytes accessed | tf_op | source)
XLA Modules:
  0.0 332.1 jit_solution(14820557727270067764)
XLA Ops:
  8.9 2.2 gather_fusion.2
  11.1 0.9 broadcast_select_fusion
  12.8 1.1 constant_dynamic-slice_fusion.1
  13.9 3.0 collective-permute-start
  16.9 15.0 %collective-permute-done = bf16[1024,256]{1,0:T(8,128)(2,1)S(1)} collective-permute-done((bf16[1024,256]{1,0:T(8,128)(2,1)S(1)}, bf16[1024,256]{1,0:T(8,128)(2,1)S(1)}, u32[]{:S(2)}, u32[]{:S(2)}) %collective-permute-start) | collective-permute-done | bytes 524320 | tf_op jit(solution)/shard_map/ppermute | solution.py:102
  31.9 15.8 %collective-permute-done.1 = bf16[1024,256]{1,0:T(8,128)(2,1)S(1)} collective-permute-done((bf16[1024,256]{1,0:T(8,128)(2,1)S(1)}, bf16[1024,256]{1,0:T(8,128)(2,1)S(1)}, u32[]{:S(2)}, u32[]{:S(2)}) %collective-permute-start.1) | collective-permute-done | bytes 524320 | tf_op jit(solution)/shard_map/ppermute | solution.py:102
  47.7 23.4 %collective-permute-done.2 = bf16[1024,256]{1,0:T(8,128)(2,1)S(1)} collective-permute-done((bf16[1024,256]{1,0:T(8,128)(2,1)S(1)}, bf16[1024,256]{1,0:T(8,128)(2,1)S(1)}, u32[]{:S(2)}, u32[]{:S(2)}) %collective-permute-start.2) | collective-permute-done | bytes 524320 | tf_op jit(solution)/shard_map/ppermute | solution.py:102
  71.0 25.8 %collective-permute-done.3 = bf16[1024,256]{1,0:T(8,128)(2,1)S(1)} collective-permute-done((bf16[1024,256]{1,0:T(8,128)(2,1)S(1)}, bf16[1024,256]{1,0:T(8,128)(2,1)S(1)}, u32[]{:S(2)}, u32[]{:S(2)}) %collective-permute-start.3) | collective-permute-done | bytes 524320 | tf_op jit(solution)/shard_map/ppermute | solution.py:102
  96.8 16.1 %collective-permute-done.4 = bf16[1024,256]{1,0:T(8,128)(2,1)S(1)} collective-permute-done((bf16[1024,256]{1,0:T(8,128)(2,1)S(1)}, bf16[1024,256]{1,0:T(8,128)(2,1)S(1)}, u32[]{:S(2)}, u32[]{:S(2)}) %collective-permute-start.4) | collective-permute-done | bytes 524320 | tf_op jit(solution)/shard_map/ppermute | solution.py:102
  113.0 12.6 %collective-permute-done.5 = bf16[1024,256]{1,0:T(8,128)(2,1)S(1)} collective-permute-done((bf16[1024,256]{1,0:T(8,128)(2,1)S(1)}, bf16[1024,256]{1,0:T(8,128)(2,1)S(1)}, u32[]{:S(2)}, u32[]{:S(2)}) %collective-permute-start.5) | collective-permute-done | bytes 524320 | tf_op jit(solution)/shard_map/ppermute | solution.py:102
  125.6 20.3 %collective-permute-done.6 = bf16[1024,256]{1,0:T(8,128)(2,1)} collective-permute-done((bf16[1024,256]{1,0:T(8,128)(2,1)S(1)}, bf16[1024,256]{1,0:T(8,128)(2,1)}, u32[]{:S(2)}, u32[]{:S(2)}) %collective-permute-start.6) | collective-permute-done | bytes 524320 | tf_op jit(solution)/shard_map/ppermute | solution.py:102
  145.8 1.1 constant_dynamic-update-slice_fusion.15
  147.3 1.2 constant_dynamic-update-slice_fusion.7
  148.8 2.2 constant_dynamic-slice_fusion
  152.0 0.8 copy.137
  152.9 7.9 %gather_fusion = s32[1024,4,8]{2,1,0:T(4,128)} fusion(s32[1024,4,8]{2,1,0:T(4,128)S(1)} %bitcast.100, s32[1024]{0:T(1024)S(1)} %get-tuple-element.224), kind=kCustom, calls=%fused_computation | custom fusion | bytes 266240 | tf_op jit(solution)/shard_map/gather | solution.py:12
  160.8 1.8 copy.113
  162.8 2.1 select_reduce_fusion
  165.0 1.2 select_select_fusion.1
  166.3 28.4 %while.26 = (s32[]{:T(128)}, bf16[2,512,4,256]{3,1,0,2:T(8,128)(2,1)S(1)}, s32[2,512,4,8]{1,3,2,0:T(8,128)S(1)}, bf16[4,512,256]{2,1,0:T(8,128)(2,1)}, s32[]{:T(128)}) while((s32[]{:T(128)}, bf16[2,512,4,256]{3,1,0,2:T(8,128)(2,1)S(1)}, s32[2,512,4,8]{1,3,2,0:T(8,128)S(1)}, bf16[4,512,256]{2,1,0:T(8,128)(2,1)}, s32[]{:T(128)}) %tuple.90), condition=%wide.region_3.4_spmd.clone, body=%wide.region_1.3_spmd.clone.sunk | while | flops 561512448 | bytes 6619205 | solution.py:24
  166.8 11.7 %fusion.60 = bf16[512,4,512]{2,1,0:T(4,128)(2,1)S(1)} fusion(s32[512,4,8]{2,1,0:T(4,128)S(1)} %copy.164), kind=kLoop, calls=%fused_computation.9.clone.1 | loop fusion | flops 24117248 | bytes 2162688 | tf_op jit(solution)/shard_map/while/body/eval_jaxpr/reduce_sum | solution.py:18
  178.5 2.1 fusion.61
  181.1 11.7 %fusion.60 = bf16[512,4,512]{2,1,0:T(4,128)(2,1)S(1)} fusion(s32[512,4,8]{2,1,0:T(4,128)S(1)} %copy.164), kind=kLoop, calls=%fused_computation.9.clone.1 | loop fusion | flops 24117248 | bytes 2162688 | tf_op jit(solution)/shard_map/while/body/eval_jaxpr/reduce_sum | solution.py:18
  192.8 2.0 fusion.61
  194.8 2.9 copy.115
  197.7 4.5 %all-to-all-start = ((bf16[1024,4,256]{2,1,0:T(4,128)(2,1)}), bf16[1024,4,256]{2,1,0:T(4,128)(2,1)}, u32[]{:S(2)}, u32[]{:S(2)}) async-start(bf16[1024,4,256]{2,1,0:T(4,128)(2,1)} %copy.115), calls=%async_computation | async-start | bytes 4194304 | tf_op jit(solution)/shard_map/all_to_all | solution.py:80
  202.2 0.8 copy.138
  203.1 7.9 %gather_fusion.1 = s32[1024,4,8]{2,1,0:T(4,128)} fusion(s32[1024,4,8]{2,1,0:T(4,128)S(1)} %bitcast.101, s32[1024]{0:T(1024)S(1)} %get-tuple-element.223), kind=kCustom, calls=%fused_computation.1 | custom fusion | bytes 266240 | tf_op jit(solution)/shard_map/gather | solution.py:12
  211.0 1.8 copy.120
  213.0 28.2 %while.27 = (s32[]{:T(128)}, bf16[2,512,4,256]{3,1,0,2:T(8,128)(2,1)S(1)}, s32[2,512,4,8]{1,3,2,0:T(8,128)S(1)}, bf16[4,512,256]{2,1,0:T(8,128)(2,1)}, s32[]{:T(128)}) while((s32[]{:T(128)}, bf16[2,512,4,256]{3,1,0,2:T(8,128)(2,1)S(1)}, s32[2,512,4,8]{1,3,2,0:T(8,128)S(1)}, bf16[4,512,256]{2,1,0:T(8,128)(2,1)}, s32[]{:T(128)}) %tuple.91), condition=%wide.region_6.7_spmd.clone, body=%wide.region_4.6_spmd.clone.sunk | while | flops 561512448 | bytes 6619205 | solution.py:24
  213.4 11.7 %fusion.64 = bf16[512,4,512]{2,1,0:T(4,128)(2,1)S(1)} fusion(s32[512,4,8]{2,1,0:T(4,128)S(1)} %copy.166), kind=kLoop, calls=%fused_computation.18.clone.1 | loop fusion | flops 24117248 | bytes 2162688 | tf_op jit(solution)/shard_map/while/body/eval_jaxpr/reduce_sum | solution.py:18
  225.1 1.9 fusion.65
  227.5 11.7 %fusion.64 = bf16[512,4,512]{2,1,0:T(4,128)(2,1)S(1)} fusion(s32[512,4,8]{2,1,0:T(4,128)S(1)} %copy.166), kind=kLoop, calls=%fused_computation.18.clone.1 | loop fusion | flops 24117248 | bytes 2162688 | tf_op jit(solution)/shard_map/while/body/eval_jaxpr/reduce_sum | solution.py:18
  239.3 1.9 fusion.65
  241.2 3.0 copy.122
  244.2 1.4 all-to-all-done
  245.6 4.3 %all-to-all-start.1 = ((bf16[1024,4,256]{2,1,0:T(4,128)(2,1)}), bf16[1024,4,256]{2,1,0:T(4,128)(2,1)S(1)}, u32[]{:S(2)}, u32[]{:S(2)}) async-start(bf16[1024,4,256]{2,1,0:T(4,128)(2,1)} %copy.122), calls=%async_computation.1 | async-start | bytes 4194304 | tf_op jit(solution)/shard_map/all_to_all | solution.py:80
  250.8 1.4 gather_fusion.4
  253.2 1.1 slice_bitcast_fusion.1
  254.2 3.3 select_select_fusion
  257.5 1.9 copy.116
  259.4 1.5 copy.117
  260.9 36.4 %all-to-all-done.1 = bf16[1024,4,256]{2,1,0:T(4,128)(2,1)S(1)} async-done(((bf16[1024,4,256]{2,1,0:T(4,128)(2,1)}), bf16[1024,4,256]{2,1,0:T(4,128)(2,1)S(1)}, u32[]{:S(2)}, u32[]{:S(2)}) %all-to-all-start.1) | async-done | bytes 2097184 | tf_op jit(solution)/shard_map/all_to_all | solution.py:80
  297.7 1.2 copy-done.1
  299.3 2.4 copy.125
  301.7 6.3 %copy.142 = bf16[32,8,32,256]{3,1,2,0:T(8,128)(2,1)} copy(bf16[32,8,32,256]{3,2,1,0:T(8,128)(2,1)S(1)} %bitcast.99) | data formatting | bytes 8388608
  308.0 4.1 %convolution_convert_fusion = bf16[256,128]{1,0:T(8,128)(2,1)S(1)} fusion(bf16[256,8192]{1,0:T(8,128)(2,1)} %bitcast.97, bf16[8192,128]{1,0:T(8,128)(2,1)} %all-gather.7.cloned.1.call-done), kind=kOutput, calls=%fused_computation.35 | convolution fusion | flops 536903680 | bytes 6356992 | tf_op jit(solution)/shard_map/dot_general | solution.py:84
  312.3 12.7 %fusion.33 = f32[256]{0:T(256)S(1)} fusion(bf16[8192,1024]{1,0:T(8,128)(2,1)} %all-gather.11.cloned.1.call-done, bf16[256,128]{1,0:T(8,128)(2,1)S(1)} %convolution_convert_fusion, bf16[128,8192]{1,0:T(8,128)(2,1)} %all-gather.9.cloned.1.call-done, bf16[256,8192]{1,0:T(8,128)(2,1)} %bitcast.98, f32[8192]{0:T(1024)S(1)} %copy-done.9, ...), kind=kOutput, calls=%fused_computation.34 | convolution fusion | flops 4843372544 | bytes 23176192 | tf_op jit(solution)/shard_map/dot_general | solution.py:108
  (91 shorter events, 8.8 us)
Async XLA Ops:
  7.2 245.0 %copy-start = (s32[4,4]{1,0:T(4,128)S(1)}, s32[4,4]{1,0:T(4,128)}, u32[]{:S(2)}) copy-start(s32[4,4]{1,0:T(4,128)} %param.20) | copy-start | bytes 196
  7.2 155.6 %all-gather.5.cloned.1.call-start = ((), (), s32[]{:S(2)}) async-start(), calls=%async_computation.2 | async-start | bytes 2621440 | tf_op jit(solution)/shard_map/all_gather | solution.py:56
  12.0 296.0 %all-gather.7.cloned.1.call-start = ((), (), s32[]{:S(2)}) async-start(), calls=%async_computation.3 | async-start | bytes 2359296 | tf_op jit(solution)/shard_map/all_gather | solution.py:86
  12.8 299.4 %all-gather.9.cloned.1.call-start = ((), (), s32[]{:S(2)}) async-start(), calls=%async_computation.4 | async-start | bytes 2359296 | tf_op jit(solution)/shard_map/all_gather | solution.py:92
  13.9 18.0 %collective-permute-start = (bf16[1024,256]{1,0:T(8,128)(2,1)S(1)}, bf16[1024,256]{1,0:T(8,128)(2,1)S(1)}, u32[]{:S(2)}, u32[]{:S(2)}) collective-permute-start(bf16[1024,256]{1,0:T(8,128)(2,1)S(1)} %constant_dynamic-slice_fusion.1), channel_id=1, source_target_pairs={{0,4},{4,8},{8,12},{12,16},{16,20},{20,24},{24,28},{28,0},{1,5},{5... | collective-permute-start | bytes 1572872 | tf_op jit(solution)/shard_map/ppermute | solution.py:102
  31.9 15.8 %collective-permute-start.1 = (bf16[1024,256]{1,0:T(8,128)(2,1)S(1)}, bf16[1024,256]{1,0:T(8,128)(2,1)S(1)}, u32[]{:S(2)}, u32[]{:S(2)}) collective-permute-start(bf16[1024,256]{1,0:T(8,128)(2,1)S(1)} %collective-permute-done), channel_id=1, source_target_pairs={{0,4},{4,8},{8,12},{12,16},{16,20},{20,24},{24,28},{28,0},{1,5},{5... | collective-permute-start | bytes 1572872 | tf_op jit(solution)/shard_map/ppermute | solution.py:102
  47.7 23.4 %collective-permute-start.2 = (bf16[1024,256]{1,0:T(8,128)(2,1)S(1)}, bf16[1024,256]{1,0:T(8,128)(2,1)S(1)}, u32[]{:S(2)}, u32[]{:S(2)}) collective-permute-start(bf16[1024,256]{1,0:T(8,128)(2,1)S(1)} %collective-permute-done.1), channel_id=1, source_target_pairs={{0,4},{4,8},{8,12},{12,16},{16,20},{20,24},{24,28},{28,0},{1,5},{5... | collective-permute-start | bytes 1572872 | tf_op jit(solution)/shard_map/ppermute | solution.py:102
  71.0 25.8 %collective-permute-start.3 = (bf16[1024,256]{1,0:T(8,128)(2,1)S(1)}, bf16[1024,256]{1,0:T(8,128)(2,1)S(1)}, u32[]{:S(2)}, u32[]{:S(2)}) collective-permute-start(bf16[1024,256]{1,0:T(8,128)(2,1)S(1)} %collective-permute-done.2), channel_id=1, source_target_pairs={{0,4},{4,8},{8,12},{12,16},{16,20},{20,24},{24,28},{28,0},{1,5},{5... | collective-permute-start | bytes 1572872 | tf_op jit(solution)/shard_map/ppermute | solution.py:102
  96.8 16.1 %collective-permute-start.4 = (bf16[1024,256]{1,0:T(8,128)(2,1)S(1)}, bf16[1024,256]{1,0:T(8,128)(2,1)S(1)}, u32[]{:S(2)}, u32[]{:S(2)}) collective-permute-start(bf16[1024,256]{1,0:T(8,128)(2,1)S(1)} %collective-permute-done.3), channel_id=1, source_target_pairs={{0,4},{4,8},{8,12},{12,16},{16,20},{20,24},{24,28},{28,0},{1,5},{5... | collective-permute-start | bytes 1572872 | tf_op jit(solution)/shard_map/ppermute | solution.py:102
  112.9 12.6 %collective-permute-start.5 = (bf16[1024,256]{1,0:T(8,128)(2,1)S(1)}, bf16[1024,256]{1,0:T(8,128)(2,1)S(1)}, u32[]{:S(2)}, u32[]{:S(2)}) collective-permute-start(bf16[1024,256]{1,0:T(8,128)(2,1)S(1)} %collective-permute-done.4), channel_id=1, source_target_pairs={{0,4},{4,8},{8,12},{12,16},{16,20},{20,24},{24,28},{28,0},{1,5},{5... | collective-permute-start | bytes 1572872 | tf_op jit(solution)/shard_map/ppermute | solution.py:102
  113.0 199.3 %all-gather.11.cloned.1.call-start = ((), (), s32[]{:S(2)}) async-start(), calls=%async_computation.5 | async-start | bytes 20971520 | tf_op jit(solution)/shard_map/all_gather | solution.py:110
  125.6 20.3 %collective-permute-start.6 = (bf16[1024,256]{1,0:T(8,128)(2,1)S(1)}, bf16[1024,256]{1,0:T(8,128)(2,1)}, u32[]{:S(2)}, u32[]{:S(2)}) collective-permute-start(bf16[1024,256]{1,0:T(8,128)(2,1)S(1)} %collective-permute-done.5), channel_id=1, source_target_pairs={{0,4},{4,8},{8,12},{12,16},{16,20},{20,24},{24,28},{28,0},{1,5},{5... | collective-permute-start | bytes 1572872 | tf_op jit(solution)/shard_map/ppermute | solution.py:102
  125.6 21.6 %copy-start.4 = (bf16[1024,1024]{1,0:T(8,128)(2,1)S(1)}, bf16[1024,1024]{1,0:T(8,128)(2,1)}, u32[]{:S(2)}) copy-start(bf16[1024,1024]{1,0:T(8,128)(2,1)} %param.28) | copy-start | bytes 6291460
  151.0 0.7 copy-start.6
  151.0 1.0 copy-start.5
  151.0 1.8 copy-start.7
  152.0 10.7 %copy-start.8 = (s32[4,2]{0,1:T(2,128)S(1)}, s32[4,2]{0,1:T(2,128)}, u32[]{:S(2)}) copy-start(s32[4,2]{0,1:T(2,128)} %param.22) | copy-start | bytes 100
  152.9 12.1 %copy-start.2 = (bf16[4,4,128,256]{3,2,1,0:T(8,128)(2,1)S(1)}, bf16[4,4,128,256]{3,2,1,0:T(8,128)(2,1)}, u32[]{:S(2)}) copy-start(bf16[4,4,128,256]{3,2,1,0:T(8,128)(2,1)} %param.18) | copy-start | bytes 3145732
  197.7 47.9 %all-to-all-start = ((bf16[1024,4,256]{2,1,0:T(4,128)(2,1)}), bf16[1024,4,256]{2,1,0:T(4,128)(2,1)}, u32[]{:S(2)}, u32[]{:S(2)}) async-start(bf16[1024,4,256]{2,1,0:T(4,128)(2,1)} %copy.115), calls=%async_computation | async-start | bytes 4194304 | tf_op jit(solution)/shard_map/all_to_all | solution.py:80
  241.2 9.5 %copy-start.3 = (bf16[4,4,128,256]{3,2,1,0:T(8,128)(2,1)S(1)}, bf16[4,4,128,256]{3,2,1,0:T(8,128)(2,1)}, u32[]{:S(2)}) copy-start(bf16[4,4,128,256]{3,2,1,0:T(8,128)(2,1)} %param.18) | copy-start | bytes 3145732
  245.6 51.7 %all-to-all-start.1 = ((bf16[1024,4,256]{2,1,0:T(4,128)(2,1)}), bf16[1024,4,256]{2,1,0:T(4,128)(2,1)S(1)}, u32[]{:S(2)}, u32[]{:S(2)}) async-start(bf16[1024,4,256]{2,1,0:T(4,128)(2,1)} %copy.122), calls=%async_computation.1 | async-start | bytes 4194304 | tf_op jit(solution)/shard_map/all_to_all | solution.py:80
  297.3 1.6 copy-start.1
  308.0 4.2 %copy-start.9 = (f32[8192]{0:T(1024)S(1)}, f32[8192]{0:T(1024)}, u32[]{:S(2)}) copy-start(f32[8192]{0:T(1024)} %param.27) | copy-start | bytes 98308
  308.0 4.2 %copy-start.10 = (f32[1024]{0:T(1024)S(1)}, f32[1024]{0:T(1024)}, u32[]{:S(2)}) copy-start(f32[1024]{0:T(1024)} %param.30) | copy-start | bytes 12292
  308.0 4.2 %copy-start.11 = (f32[1024]{0:T(1024)S(1)}, f32[1024]{0:T(1024)}, u32[]{:S(2)}) copy-start(f32[1024]{0:T(1024)} %param.29) | copy-start | bytes 12292
Sparse Core Ops, SparseCore 0:
  12.1 25.2 all-gather.4
  39.6 65.4 all-gather.6
  113.1 56.9 all-gather.8
  171.5 106.6 all-gather.10
